TPU v7x, 256 devices: a whole 4x4x8 slice. The times are simulated.
256 devices in a mesh: row: 16 (over z, core), col: 8 (over x, y_lo), vec: 2 (over y_hi).
Axes of the slice: x: 4, y: 4 (y_hi: 2, y_lo: 2; y = y_hi * 2 + y_lo), z: 8, core: 2. Of those that a mesh axis runs over, the one named last changes fastest.
Arguments:
- vectors: bfloat16 [16, 131072], P('vec', ('row', 'col')), may hold values from -6 to 6
- tile_vals: bfloat16 [16, 8, 256, 128, 128], P('row', 'col'), may hold values from -0.09375 to 0.09375
- tile_rows: int32 [16, 8, 256], P('row', 'col'), may hold values from 0 to 1023, as said below
- tile_cols: int32 [16, 8, 256], P('row', 'col'), may hold values from 0 to 1023, as said below
- tile_counts: int32 [16, 8], P('row', 'col'), may hold values from 1 to 256, as said below
Outputs:
- product: bfloat16 [16, 131072], P('vec', ('row', 'col'))
- gram: float32 [16, 16], P(None, 'vec')
Inputs may be any that keep to these rules, and one draw needn't show every extreme that they name: `tile_rows`: list [i, j] names tiles whose row index r has i * 64 <= r < (i + 1) * 64 and whose column index c has (c // 8) % (8) == j, that is the column's block of 8 tile rows, numbered c // 8, is held by column group j; live slots name distinct tiles with r >= c; slots at or beyond the count hold in-range indices that must be ignored. `tile_cols`: see tile_rows; the same slots. `tile_counts`: some lists are full in every draw; lists near the top of the triangle hold few tiles.
All inputs are finite; a program needn't handle non-finite values.
Results may differ from a plain program's by a relative error of at most 0.001.
Values may be sent and summed in bfloat16 or wider, within the bound.
A program may use at most 64 MiB of HBM per device.

v0:
```python
import math
import jax
import jax.numpy as jnp
from jax import lax
from jax.sharding import PartitionSpec as P


def shards(vectors, tile_vals, tile_rows, tile_cols, tile_counts):
    nrow = lax.axis_size("row")
    ncol = lax.axis_size("col")
    vlocal, width = vectors.shape
    tile = tile_vals.shape[-1]
    stretch = width // tile
    span = ncol * stretch
    colspan = nrow * stretch
    row_x = lax.all_gather(vectors, "col", axis=1, tiled=True)
    col_x = lax.all_gather(vectors, "row", axis=1, tiled=True)
    tiles = tile_vals[0, 0]
    rows = tile_rows[0, 0]
    cols = tile_cols[0, 0]
    count = tile_counts[0, 0]
    slots = jnp.arange(rows.shape[0], dtype=jnp.int32)
    live = slots < count
    mirror = live & (rows != cols)
    row_place = rows % span
    col_place = cols // span * stretch + cols % stretch
    row_blocks = row_x.reshape(vlocal, span, tile)
    col_blocks = col_x.reshape(vlocal, colspan, tile)
    picked_cols = jnp.take(col_blocks, col_place, axis=1)
    picked_rows = jnp.take(row_blocks, row_place, axis=1)
    down = jnp.einsum("tij,vtj->vti", tiles, picked_cols, preferred_element_type=jnp.float32)
    upper = jnp.einsum("tij,vti->vtj", tiles, picked_rows, preferred_element_type=jnp.float32)
    row_hit = (
        (row_place[None, :] == jnp.arange(span, dtype=jnp.int32)[:, None]) & live[None, :]
    ).astype(jnp.float32)
    col_hit = (
        (col_place[None, :] == jnp.arange(colspan, dtype=jnp.int32)[:, None]) & mirror[None, :]
    ).astype(jnp.float32)
    row_part = jnp.einsum("at,vti->vai", row_hit, down, precision=lax.Precision.HIGHEST).reshape(
        vlocal, span * tile
    )
    col_part = jnp.einsum("at,vti->vai", col_hit, upper, precision=lax.Precision.HIGHEST).reshape(
        vlocal, colspan * tile
    )
    row_whole = lax.psum(row_part, "col")
    col_whole = lax.psum(col_part, "row")
    row_share = lax.dynamic_slice_in_dim(row_whole, lax.axis_index("col") * width, width, 1)
    col_share = lax.dynamic_slice_in_dim(col_whole, lax.axis_index("row") * width, width, 1)
    image = row_share + col_share
    every_vector = lax.all_gather(vectors, "vec", axis=0, tiled=True)
    partial_gram = jnp.dot(
        every_vector.astype(jnp.float32), image.T, precision=lax.Precision.HIGHEST
    )
    gram = lax.psum(partial_gram, ("row", "col")) / math.sqrt(width * nrow * ncol)
    return (image.astype(jnp.bfloat16), gram)


def solution(mesh):
    return jax.shard_map(
        shards,
        mesh=mesh,
        in_specs=(
            P("vec", ("row", "col")),
            P("row", "col", None, None, None),
            P("row", "col", None),
            P("row", "col", None),
            P("row", "col"),
        ),
        out_specs=(P("vec", ("row", "col")), P(None, "vec")),
        check_vma=False,
    )
```

profile of v0, /device:TPU:8, one launch (start us, length us, event | category | flops | bytes accessed | tf_op | source)
XLA Modules:
  0.0 527.4 jit_solution(8425430569256399796)
XLA Ops:
  7.2 0.0 copy-start.1
  7.2 0.0 copy-start.2
  7.2 0.0 all-reduce.5.cloned.1.call-start
  7.2 28.5 %all_gather.10 = bf16[8,8192]{1,0:T(8,128)(2,1)S(1)} all-gather(bf16[8,1024]{1,0:T(8,128)(2,1)} %param.5), channel_id=1, replica_groups=mesh['row'=16,'col'=8,'vec'=2] {'col'}, dimensions={1}, use_global_device_ids=true | all-gather | bytes 147456 | tf_op jit(solution)/shard_map/all_gather | solution.py:16
  35.8 0.7 compare_select_fusion
  36.5 0.7 compare_and_fusion.1
  37.2 0.8 gather_fusion.1
  38.0 0.0 copy-start
  38.0 4.7 fusion
  42.7 0.4 copy.9
  43.8 0.0 copy-done.1
  43.8 0.0 copy-done.2
  43.8 0.6 convolution_bitcast_fusion
  44.5 0.2 copy.7
  44.7 1.1 copy.18
  45.8 0.0 all-reduce.5.cloned.1.call-update
  45.8 0.0 all-reduce.3.cloned.1.call-start
  45.9 0.0 copy-done
  45.9 20.7 %all_gather.9 = bf16[8,16384]{1,0:T(8,128)(2,1)S(1)} all-gather(bf16[8,1024]{1,0:T(8,128)(2,1)S(1)} %copy-done), channel_id=1, replica_groups=mesh['row'=16,'col'=8,'vec'=2] {'row'}, dimensions={1}, use_global_device_ids=true | all-gather | bytes 278528 | tf_op jit(solution)/shard_map/all_gather | solution.py:17
  66.6 0.8 gather_fusion
  67.4 6.8 %fusion.2 = f32[256,8,128]{2,1,0:T(8,128)S(1)} fusion(bf16[1,1,256,128,128]{4,3,2,1,0:T(8,128)(2,1)} %param.6, bf16[256,8,128]{2,1,0:T(8,128)(2,1)S(1)} %gather_fusion, pred[256]{0:T(512)(128)(4,1)S(1)} %get-tuple-element.2), kind=kOutput, calls=%fused_computation.4 | convolution fusion | flops 67371008 | bytes 9961728 | tf_op jit(solution)/shard_map/tij,vtj->vti/dot_general | solution.py:31
  74.2 0.6 convolution_bitcast_fusion.1
  74.8 0.9 copy.19
  75.7 0.0 all-reduce.3.cloned.1.call-update
  75.7 5.9 %all_gather.11 = bf16[16,1024]{1,0:T(8,128)(2,1)S(1)} all-gather(bf16[8,1024]{1,0:T(8,128)(2,1)S(1)} %copy-done), channel_id=1, replica_groups=mesh['row'=16,'col'=8,'vec'=2] {'vec'}, dimensions={0}, use_global_device_ids=true | all-gather | bytes 49152 | tf_op jit(solution)/shard_map/all_gather | solution.py:50
  81.7 77.3 %all-reduce.5.cloned.1.call-done = f32[8,16384]{1,0:T(8,128)} async-done(((f32[8,16384]{1,0:T(8,128)}), f32[8,16384]{1,0:T(8,128)}) %all-reduce.5.cloned.1.call-update) | async-done | bytes 524304 | tf_op jit(solution)/shard_map/psum | solution.py:46
  159.0 79.9 %all-reduce.3.cloned.1.call-done = f32[8,8192]{1,0:T(8,128)} async-done(((f32[8,8192]{1,0:T(8,128)}), f32[8,8192]{1,0:T(8,128)}) %all-reduce.3.cloned.1.call-update) | async-done | bytes 262160 | tf_op jit(solution)/shard_map/psum | solution.py:45
  238.9 0.9 convolution_bitcast_fusion.2
  239.8 278.8 %psum.23 = f32[16,8]{0,1:T(8,128)S(1)} all-reduce(f32[16,8]{0,1:T(8,128)S(1)} %convolution_bitcast_fusion.2), channel_id=1, replica_groups=mesh['row'=16,'col'=8,'vec'=2] {'row','col'}, use_global_device_ids=true, to_apply=%region_2.3 | all-reduce | flops 128 | bytes 1024 | tf_op jit(solution)/shard_map/psum | solution.py:54
  518.6 0.6 broadcast_multiply_fusion
  519.2 1.4 fusion.25
  (5 shorter events, 0.1 us)
Async XLA Ops:
  7.2 36.6 %copy-start.1 = (s32[1,1,256]{2,1,0:T(1,128)S(1)}, s32[1,1,256]{2,1,0:T(1,128)}, u32[]{:S(2)}) copy-start(s32[1,1,256]{2,1,0:T(1,128)} %param.7) | copy-start | bytes 3076
  7.2 36.6 %copy-start.2 = (s32[1,1,256]{2,1,0:T(1,128)S(1)}, s32[1,1,256]{2,1,0:T(1,128)}, u32[]{:S(2)}) copy-start(s32[1,1,256]{2,1,0:T(1,128)} %param.8) | copy-start | bytes 3076
  7.2 151.8 %all-reduce.5.cloned.1.call-start = ((), (), s32[]{:S(2)}) async-start(), calls=%async_computation.1 | async-start | bytes 1048576 | tf_op jit(solution)/shard_map/psum | solution.py:46
  38.0 7.9 %copy-start = (bf16[8,1024]{1,0:T(8,128)(2,1)S(1)}, bf16[8,1024]{1,0:T(8,128)(2,1)}, u32[]{:S(2)}) copy-start(bf16[8,1024]{1,0:T(8,128)(2,1)} %param.5) | copy-start | bytes 49156
  45.8 193.1 %all-reduce.3.cloned.1.call-start = ((), (), s32[]{:S(2)}) async-start(), calls=%async_computation | async-start | bytes 524288 | tf_op jit(solution)/shard_map/psum | solution.py:45
Sparse Core Ops, SparseCore 0:
  45.9 113.0 all-reduce.4
  161.6 77.2 all-reduce.2
where the time goes:
time: 528 us; the launch traced here: 527 us
  blocking collectives  334 us (63%)
  waiting for transfers between devices  157 us (30%)
  between operations  14.8 us (3%)
  matrix products  13.7 us (3%)
    psum x1, blocking collectives, shards(): lax.psum(partial_gram, ('row', 'col')) / math.sqrt(width * nrow * ncol)  279 us
    psum x1, waiting for transfers between devices, shards(): row_whole = lax.psum(row_part, 'col')  79.9 us
    psum x1, waiting for transfers between devices, shards(): col_whole = lax.psum(col_part, 'row')  77.3 us
    all_gather x1, blocking collectives, shards(): row_x = lax.all_gather(vectors, 'col', axis=1, tiled=True)  28.5 us
    all_gather x1, blocking collectives, shards(): col_x = lax.all_gather(vectors, 'row', axis=1, tiled=True)  20.7 us
  transfers between devices with their start and end apart: 2, of which 2 were waited for; matrix products, arithmetic and copies ran while one was open for 2% of the time, Pallas kernels for 0%

commit v1 on v0

--- a/solution.py
+++ b/solution.py
@@ -51,7 +51,13 @@
     partial_gram = jnp.dot(
         every_vector.astype(jnp.float32), image.T, precision=lax.Precision.HIGHEST
     )
-    gram = lax.psum(partial_gram, ("row", "col")) / math.sqrt(width * nrow * ncol)
+
+    def rows_play(arr_in):
+        for no in ("col", "row"):
+            arr_in = lax.psum(arr_in, no)
+        return arr_in
+
+    gram = rows_play(partial_gram) / math.sqrt(width * nrow * ncol)
     return (image.astype(jnp.bfloat16), gram)
 
 

time: 528 us -> 294 us (0.56)
  blocking collectives: 334 us -> 97.5 us
    psum x1 -> x2, blocking collectives: 279 us -> 42.4 us  [rows_play(): arr_in = lax.psum(arr_in, no)]
  transfers between devices with their start and end apart: 2 -> 2, of which waited for: 2 -> 2; matrix products, arithmetic and copies ran while one was open for 2% -> 3% of each run, Pallas kernels for 0% -> 0%
where the time goes in v1:
time: 294 us; the launch traced here: 291 us
  waiting for transfers between devices  157 us (53%)
  blocking collectives  97.5 us (33%)
  between operations  14.8 us (5%)
  matrix products  13.7 us (5%)
  local copies, waits for them, and re-layouts  4.24 us (1%)
  other arithmetic  3.42 us (1%)
    psum x1, waiting for transfers between devices, shards(): row_whole = lax.psum(row_part, 'col')  79.9 us
    psum x1, waiting for transfers between devices, shards(): col_whole = lax.psum(col_part, 'row')  77.3 us
    psum x2, blocking collectives, rows_play(): arr_in = lax.psum(arr_in, no)  42.4 us
    all_gather x1, blocking collectives, shards(): row_x = lax.all_gather(vectors, 'col', axis=1, tiled=True)  28.5 us
    all_gather x1, blocking collectives, shards(): col_x = lax.all_gather(vectors, 'row', axis=1, tiled=True)  20.7 us
    dot_general x1, matrix products, shards(): jnp.einsum('tij,vtj->vti', tiles, picked_cols, preferred_element_type=jnp...  6.82 us
    all_gather x1, blocking collectives, shards(): every_vector = lax.all_gather(vectors, 'vec', axis=0, tiled=True)  5.91 us
  transfers between devices with their start and end apart: 2, of which 2 were waited for; matrix products, arithmetic and copies ran while one was open for 3% of the time, Pallas kernels for 0%

profile of v1, /device:TPU:8, one launch (start us, length us, event | category | flops | bytes accessed | tf_op | source)
XLA Modules:
  0.0 291.0 jit_solution(14123897199318023767)
XLA Ops:
  7.2 0.0 copy-start.1
  7.2 0.0 copy-start.2
  7.2 0.0 all-reduce.5.cloned.1.call-start
  7.2 28.5 %all_gather.10 = bf16[8,8192]{1,0:T(8,128)(2,1)S(1)} all-gather(bf16[8,1024]{1,0:T(8,128)(2,1)} %param.5), channel_id=1, replica_groups=mesh['row'=16,'col'=8,'vec'=2] {'col'}, dimensions={1}, use_global_device_ids=true | all-gather | bytes 147456 | tf_op jit(solution)/shard_map/all_gather | solution.py:16
  35.8 0.7 compare_select_fusion
  36.5 0.7 compare_and_fusion.1
  37.2 0.8 gather_fusion.1
  38.0 0.0 copy-start
  38.0 4.7 %fusion = f32[256,8,128]{2,1,0:T(8,128)S(1)} fusion(bf16[1,1,256,128,128]{4,3,2,1,0:T(8,128)(2,1)} %param.6, bf16[256,8,128]{2,1,0:T(8,128)(2,1)S(1)} %gather_fusion.1, pred[256]{0:T(512)(128)(4,1)S(1)} %get-tuple-element.4), kind=kOutput, calls=%fused_computation.2 | convolution fusion | flops 67371008 | bytes 9961728 | tf_op jit(solution)/shard_map/tij,vti->vtj/dot_general | solution.py:32
  42.7 0.4 copy.9
  43.8 0.0 copy-done.1
  43.8 0.0 copy-done.2
  43.8 0.6 convolution_bitcast_fusion
  44.5 0.2 copy.7
  44.7 1.1 copy.18
  45.8 0.0 all-reduce.5.cloned.1.call-update
  45.8 0.0 all-reduce.3.cloned.1.call-start
  45.9 0.0 copy-done
  45.9 20.7 %all_gather.9 = bf16[8,16384]{1,0:T(8,128)(2,1)S(1)} all-gather(bf16[8,1024]{1,0:T(8,128)(2,1)S(1)} %copy-done), channel_id=1, replica_groups=mesh['row'=16,'col'=8,'vec'=2] {'row'}, dimensions={1}, use_global_device_ids=true | all-gather | bytes 278528 | tf_op jit(solution)/shard_map/all_gather | solution.py:17
  66.6 0.8 gather_fusion
  67.4 6.8 %fusion.2 = f32[256,8,128]{2,1,0:T(8,128)S(1)} fusion(bf16[1,1,256,128,128]{4,3,2,1,0:T(8,128)(2,1)} %param.6, bf16[256,8,128]{2,1,0:T(8,128)(2,1)S(1)} %gather_fusion, pred[256]{0:T(512)(128)(4,1)S(1)} %get-tuple-element.2), kind=kOutput, calls=%fused_computation.4 | convolution fusion | flops 67371008 | bytes 9961728 | tf_op jit(solution)/shard_map/tij,vtj->vti/dot_general | solution.py:31
  74.2 0.6 convolution_bitcast_fusion.1
  74.9 0.9 copy.19
  75.7 0.0 all-reduce.3.cloned.1.call-update
  75.8 5.9 %all_gather.11 = bf16[16,1024]{1,0:T(8,128)(2,1)S(1)} all-gather(bf16[8,1024]{1,0:T(8,128)(2,1)S(1)} %copy-done), channel_id=1, replica_groups=mesh['row'=16,'col'=8,'vec'=2] {'vec'}, dimensions={0}, use_global_device_ids=true | all-gather | bytes 49152 | tf_op jit(solution)/shard_map/all_gather | solution.py:50
  81.7 77.3 %all-reduce.5.cloned.1.call-done = f32[8,16384]{1,0:T(8,128)} async-done(((f32[8,16384]{1,0:T(8,128)}), f32[8,16384]{1,0:T(8,128)}) %all-reduce.5.cloned.1.call-update) | async-done | bytes 524304 | tf_op jit(solution)/shard_map/psum | solution.py:46
  159.0 79.9 %all-reduce.3.cloned.1.call-done = f32[8,8192]{1,0:T(8,128)} async-done(((f32[8,8192]{1,0:T(8,128)}), f32[8,8192]{1,0:T(8,128)}) %all-reduce.3.cloned.1.call-update) | async-done | bytes 262160 | tf_op jit(solution)/shard_map/psum | solution.py:45
  238.9 0.9 convolution_bitcast_fusion.2
  239.8 18.9 %psum.30 = f32[16,8]{0,1:T(8,128)S(1)} all-reduce(f32[16,8]{0,1:T(8,128)S(1)} %convolution_bitcast_fusion.2), channel_id=1, replica_groups=mesh['row'=16,'col'=8,'vec'=2] {'col'}, use_global_device_ids=true, to_apply=%region_2.3 | all-reduce | flops 128 | bytes 1024 | tf_op jit(solution)/shard_map/psum | solution.py:57
  258.7 23.5 %psum.31 = f32[16,8]{0,1:T(8,128)S(1)} all-reduce(f32[16,8]{0,1:T(8,128)S(1)} %psum.30), channel_id=1, replica_groups=mesh['row'=16,'col'=8,'vec'=2] {'row'}, use_global_device_ids=true, to_apply=%region_3.4 | all-reduce | flops 128 | bytes 1024 | tf_op jit(solution)/shard_map/psum | solution.py:57
  282.2 0.6 broadcast_multiply_fusion
  282.8 1.4 fusion.25
  (5 shorter events, 0.1 us)
Async XLA Ops:
  7.2 36.6 %copy-start.1 = (s32[1,1,256]{2,1,0:T(1,128)S(1)}, s32[1,1,256]{2,1,0:T(1,128)}, u32[]{:S(2)}) copy-start(s32[1,1,256]{2,1,0:T(1,128)} %param.7) | copy-start | bytes 3076
  7.2 36.6 %copy-start.2 = (s32[1,1,256]{2,1,0:T(1,128)S(1)}, s32[1,1,256]{2,1,0:T(1,128)}, u32[]{:S(2)}) copy-start(s32[1,1,256]{2,1,0:T(1,128)} %param.8) | copy-start | bytes 3076
  7.2 151.8 %all-reduce.5.cloned.1.call-start = ((), (), s32[]{:S(2)}) async-start(), calls=%async_computation.1 | async-start | bytes 1048576 | tf_op jit(solution)/shard_map/psum | solution.py:46
  38.0 7.9 %copy-start = (bf16[8,1024]{1,0:T(8,128)(2,1)S(1)}, bf16[8,1024]{1,0:T(8,128)(2,1)}, u32[]{:S(2)}) copy-start(bf16[8,1024]{1,0:T(8,128)(2,1)} %param.5) | copy-start | bytes 49156
  45.8 193.1 %all-reduce.3.cloned.1.call-start = ((), (), s32[]{:S(2)}) async-start(), calls=%async_computation | async-start | bytes 524288 | tf_op jit(solution)/shard_map/psum | solution.py:45
Sparse Core Ops, SparseCore 0:
  45.9 113.0 all-reduce.4
  161.6 77.2 all-reduce.2
